TPU v7x, 256 devices: a whole 4x4x8 slice. The times are simulated.
256 devices in a mesh: req: 64 (over x, z, y_lo), kv: 4 (over y_hi, core).
Axes of the slice: x: 4, y: 4 (y_hi: 2, y_lo: 2; y = y_hi * 2 + y_lo), z: 8, core: 2. Of those that a mesh axis runs over, the one named last changes fastest.
Arguments:
- hidden: bfloat16 [64, 1024, 1536], P('req', 'kv'), may hold values from -6 to 6
- lengths: int32 [64], P('req'), may hold values from 1 to 2048, as said below
- key_cache: bfloat16 [64, 2048, 768], P('req', 'kv'), may hold values from -180 to 180
- value_cache: bfloat16 [64, 2048, 768], P('req', 'kv'), may hold values from -6 to 6
- norm_gain: bfloat16 [1536], replicated, may hold values from 0.099609375 to 1.8984375
- w_query: bfloat16 [1536, 1536], P('req', 'kv'), may hold values from -0.15625 to 0.15625
- w_key: bfloat16 [1536, 768], P('req', 'kv'), may hold values from -0.15625 to 0.15625
- w_value: bfloat16 [1536, 768], P('req', 'kv'), may hold values from -0.15625 to 0.15625
- w_out: bfloat16 [1536, 1536], P('req', 'kv'), may hold values from -0.15625 to 0.15625
Outputs:
- attended: bfloat16 [64, 1024, 1536], P('req', 'kv')
- new_keys: bfloat16 [64, 1024, 768], P('req', 'kv')
- new_values: bfloat16 [64, 1024, 768], P('req', 'kv')
Inputs may be any that keep to these rules, and one draw needn't show every extreme that they name: `lengths`: at least a quarter of the requests (one or more) hold more than 1792 tokens, one of them exactly 2048; the others hold fewer than 512.
All inputs are finite; a program needn't handle non-finite values.
Results may differ from a plain program's by a relative error of at most 0.011.
Values may be sent and summed in bfloat16 or wider, within the bound.
A program may use at most 192 MiB of HBM per device.

v0:
```python
import jax
import jax.numpy as jnp
from jax import lax
from jax.sharding import PartitionSpec as P

H = 16
KVH = 8
HD = 96
rope_base = 100000.0
masked_score = -1e30


def rms_norm(states, gain):
    mean_square = jnp.mean(states * states, axis=-1, keepdims=True)
    scaled = states * lax.rsqrt(mean_square + 1e-05) * gain.astype(jnp.float32)
    return scaled.astype(jnp.bfloat16)


def rotate(values, positions):
    count = values.shape[0]
    heads = values.shape[1] // HD
    half = HD // 2
    frequency = rope_base ** (-(jnp.arange(half, dtype=jnp.float32) * 2.0 / HD))
    angle = positions[:, None] * frequency[None, :]
    cosine = jnp.cos(angle)[:, None, :]
    sine = jnp.sin(angle)[:, None, :]
    shaped = values.reshape(count, heads, HD)
    first = shaped[..., :half]
    second = shaped[..., half:]
    turned = jnp.concatenate(
        [first * cosine - second * sine, second * cosine + first * sine], axis=-1
    )
    return turned.reshape(count, heads * HD)


def body(hidden, lengths, key_cache, value_cache, norm_gain, w_query, w_key, w_value, w_out):
    rows_here = hidden.shape[1]
    kv_count = lax.axis_size("kv")
    appended = rows_here * kv_count
    slots = key_cache.shape[1]
    groups = H // KVH
    scale = HD ** (-0.5)
    length = lengths[0]
    q_cols = w_query.shape[1]
    k_cols = w_key.shape[1]
    v_cols = w_value.shape[1]
    heads_here = q_cols // HD
    kv_heads_here = k_cols // HD
    normed = rms_norm(hidden[0].astype(jnp.float32), norm_gain)
    normed_all = lax.all_gather(normed, "kv", axis=0, tiled=True)
    pieces = jnp.concatenate([w_query, w_key, w_value, w_out], axis=1)
    cols = lax.all_gather(pieces, "req", axis=0, tiled=True)
    wq = cols[:, :q_cols]
    wk = cols[:, q_cols : q_cols + k_cols]
    wv = cols[:, q_cols + k_cols : q_cols + k_cols + v_cols]
    wo = cols[:, q_cols + k_cols + v_cols :]
    positions = (length + jnp.arange(appended, dtype=jnp.int32)).astype(jnp.float32)
    proj_q = jnp.dot(normed_all, wq, preferred_element_type=jnp.float32)
    proj_k = jnp.dot(normed_all, wk, preferred_element_type=jnp.float32)
    proj_v = jnp.dot(normed_all, wv, preferred_element_type=jnp.float32)
    queries = rotate(proj_q, positions).astype(jnp.bfloat16)
    keys_new = rotate(proj_k, positions).astype(jnp.bfloat16)
    values_new = proj_v.astype(jnp.bfloat16)
    new_keys = lax.all_to_all(keys_new, "kv", split_axis=0, concat_axis=1, tiled=True)
    new_values = lax.all_to_all(values_new, "kv", split_axis=0, concat_axis=1, tiled=True)
    keys_old = lax.all_to_all(key_cache[0], "kv", split_axis=1, concat_axis=0, tiled=True)
    values_old = lax.all_to_all(value_cache[0], "kv", split_axis=1, concat_axis=0, tiled=True)
    cache_slots = keys_old.shape[0]
    keys_all = jnp.concatenate([keys_old, keys_new], axis=0)
    values_all = jnp.concatenate([values_old, values_new], axis=0)
    key_count = keys_all.shape[0]
    query_index = jnp.arange(appended, dtype=jnp.int32)
    cache_live = jnp.arange(cache_slots, dtype=jnp.int32) < length
    visible = jnp.concatenate(
        [
            jnp.broadcast_to(cache_live[None, :], (appended, cache_slots)),
            query_index[None, :] <= query_index[:, None],
        ],
        axis=1,
    )
    query_heads = jnp.transpose(queries.reshape(appended, kv_heads_here, groups, HD), (1, 0, 2, 3))
    key_heads = jnp.transpose(keys_all.reshape(key_count, kv_heads_here, HD), (1, 0, 2))
    value_heads = jnp.transpose(values_all.reshape(key_count, kv_heads_here, HD), (1, 0, 2))

    def attend(operands):
        query_block, key_block, value_block = operands
        score = (
            jnp.einsum("qgd,kd->gqk", query_block, key_block, preferred_element_type=jnp.float32)
            * scale
        )
        score = jnp.where(visible[None], score, masked_score)
        peak = jnp.max(score, axis=-1)
        weights = jnp.where(visible[None], jnp.exp(score - peak[..., None]), 0.0)
        total = jnp.sum(weights, axis=-1)
        context = jnp.einsum(
            "gqk,kd->qgd",
            weights.astype(jnp.bfloat16),
            value_block,
            preferred_element_type=jnp.float32,
        )
        return context / jnp.transpose(total)[:, :, None]

    contexts = lax.map(attend, (query_heads, key_heads, value_heads))
    context = (
        jnp.transpose(contexts, (1, 0, 2, 3))
        .reshape(appended, heads_here * HD)
        .astype(jnp.bfloat16)
    )
    context_all = lax.all_gather(context, "kv", axis=1, tiled=True)
    attended_cols = jnp.dot(context_all, wo, preferred_element_type=jnp.float32).astype(
        jnp.bfloat16
    )
    attended = lax.all_to_all(attended_cols, "kv", split_axis=0, concat_axis=1, tiled=True)
    return (attended[None], new_keys[None], new_values[None])


def solution(mesh):
    return jax.shard_map(
        body,
        mesh=mesh,
        in_specs=(
            P("req", "kv", None),
            P("req"),
            P("req", "kv", None),
            P("req", "kv", None),
            P(),
            P("req", "kv"),
            P("req", "kv"),
            P("req", "kv"),
            P("req", "kv"),
        ),
        out_specs=(P("req", "kv", None), P("req", "kv", None), P("req", "kv", None)),
        check_vma=False,
    )
```

profile of v0, /device:TPU:1, one launch (start us, length us, event | category | flops | bytes accessed | tf_op | source)
XLA Modules:
  0.0 496.3 jit_solution(3980875130991210258)
XLA Ops:
  7.2 0.0 copy-start.11
  7.2 0.0 copy-start.13
  7.2 0.0 copy-start.14
  7.2 0.0 copy-start.12
  7.2 0.0 copy-start.7
  7.2 0.0 all-gather.4.cloned.1.call-start
  7.3 0.8 convert_element_type.52
  8.0 1.4 fusion.49
  9.5 2.3 fusion.51
  11.7 0.0 all-gather.4.cloned.1.call-update
  11.8 0.0 all-gather.6.cloned.1.call-start
  11.8 0.0 copy-done.11
  11.9 0.7 concatenate.28
  12.6 0.0 all-gather.6.cloned.1.call-update
  12.6 1.2 copy.38
  13.8 6.7 %all-to-all-start.1 = ((bf16[512,4,192]{0,2,1:T(8,128)(2,1)}), bf16[512,4,192]{0,2,1:T(8,128)(2,1)S(1)}, u32[]{:S(2)}, u32[]{:S(2)}) async-start(bf16[512,4,192]{0,2,1:T(8,128)(2,1)} %bitcast.16), calls=%async_computation.1 | async-start | bytes 1572864 | tf_op jit(solution)/shard_map/all_to_all | solution.py:66
  21.2 1.2 copy.36
  22.4 0.3 iota_compare_fusion
  22.7 1.5 multiply_cosine_fusion
  24.2 8.6 %all-to-all-done.1 = bf16[512,4,192]{0,2,1:T(8,128)(2,1)S(1)} async-done(((bf16[512,4,192]{0,2,1:T(8,128)(2,1)}), bf16[512,4,192]{0,2,1:T(8,128)(2,1)S(1)}, u32[]{:S(2)}, u32[]{:S(2)}) %all-to-all-start.1) | async-done | bytes 786464 | tf_op jit(solution)/shard_map/all_to_all | solution.py:66
  32.8 5.2 %all-to-all-start = ((bf16[512,4,192]{0,2,1:T(8,128)(2,1)}), bf16[512,4,192]{0,2,1:T(8,128)(2,1)S(1)}, u32[]{:S(2)}, u32[]{:S(2)}) async-start(bf16[512,4,192]{0,2,1:T(8,128)(2,1)} %bitcast.9), calls=%async_computation | async-start | bytes 1572864 | tf_op jit(solution)/shard_map/all_to_all | solution.py:67
  38.0 3.5 pad_add_fusion
  41.5 0.6 copy.39
  42.1 1.5 concatenate.32
  43.6 14.8 %all-to-all-done = bf16[512,4,192]{0,2,1:T(8,128)(2,1)S(1)} async-done(((bf16[512,4,192]{0,2,1:T(8,128)(2,1)}), bf16[512,4,192]{0,2,1:T(8,128)(2,1)S(1)}, u32[]{:S(2)}, u32[]{:S(2)}) %all-to-all-start) | async-done | bytes 786464 | tf_op jit(solution)/shard_map/all_to_all | solution.py:67
  58.4 0.6 copy.37
  59.0 1.5 concatenate.27
  60.5 259.1 %all-gather.6.cloned.1.call-done = bf16[1536,1152]{1,0:T(8,128)(2,1)} async-done(((bf16[24,1152]{1,0:T(8,128)(2,1)}), bf16[1536,1152]{1,0:T(8,128)(2,1)}) %all-gather.6.cloned.1.call-update) | async-done | bytes 3538960 | tf_op jit(solution)/shard_map/all_gather | solution.py:52
  319.5 3.3 fusion.55
  322.8 0.1 multiply_subtract_fusion
  323.0 2.7 fusion.53
  325.7 0.3 subtract_convert_fusion
  326.0 0.8 copy-done.1
  326.8 1.1 maximum_bitcast_fusion.1
  327.9 0.9 pad_maximum_fusion
  328.8 2.7 convolution_convert_fusion.1
  331.5 0.0 copy-start.5
  331.5 0.1 maximum_bitcast_fusion
  331.6 0.6 copy-done.5
  332.3 53.8 %while.10 = (s32[]{:T(128)}, bf16[2,1024,2,96]{1,3,2,0:T(8,128)(2,1)}, bf16[2,3072,96]{1,2,0:T(8,128)(2,1)S(1)}, pred[1024,3072]{0,1:T(8,128)(4,1)}, bf16[2,3072...) while((s32[]{:T(128)}, bf16[2,1024,2,96]{1,3,2,0:T(8,128)(2,1)}, ...), condition=%wide.region_4.5_spmd, body=%wide.region_1.4_spmd.sunk | while | flops 2453867520 | bytes 40126596 | solution.py:103
  332.3 19.3 %fusion.82 = (f32[2,1024]{1,0:T(2,128)S(1)}, bf16[2,1024,3072]{1,2,0:T(8,128)(2,1)}) fusion(pred[1024,3072]{0,1:T(8,128)(4,1)} %get-tuple-element.125, bf16[2,3072,96]{1,2,0:T(8,128)(2,1)} %get-tuple-element.126, s32[]{:T(128)} %get-tuple-element.115, bf16[2,1024,2,96]{1,3,2,0:T(8,128)(2,1)} %get-tuple-element.127), kind=kOutput, calls=%fused_computation.60.clone.1 | convolution fusion | flops 1245711360 | bytes 19866624 | tf_op jit(solution)/shard_map/while/body/eval_jaxpr/sub | solution.py:93
  351.6 6.7 %fusion.83 = bf16[2,1024,2,96]{1,3,2,0:T(8,128)(2,1)S(1)} fusion(bf16[2,1024,2,96]{1,3,2,0:T(8,128)(2,1)S(1)} %copy-done.9, s32[]{:T(128)} %get-tuple-element.115, bf16[2,1024,3072]{1,2,0:T(8,128)(2,1)} %get-tuple-element.106, bf16[2,3072,96]{1,2,0:T(8,128)(2,1)S(1)} %get-tuple-element.124, f32[1024,2]{0,1:T(2,128)S(1)} %bitcast.127), kind=kOutput, calls=%fused_computation.13.clone.1 | convolution fusion | flops 1208156160 | bytes 13968384 | tf_op jit(solution)/shard_map/while/body/eval_jaxpr/gqk,kd->qgd/dot_general | solution.py:95
  358.3 0.0 copy-start.10
  358.3 0.9 copy-done.10
  359.2 19.3 %fusion.82 = (f32[2,1024]{1,0:T(2,128)S(1)}, bf16[2,1024,3072]{1,2,0:T(8,128)(2,1)}) fusion(pred[1024,3072]{0,1:T(8,128)(4,1)} %get-tuple-element.125, bf16[2,3072,96]{1,2,0:T(8,128)(2,1)} %get-tuple-element.126, s32[]{:T(128)} %get-tuple-element.115, bf16[2,1024,2,96]{1,3,2,0:T(8,128)(2,1)} %get-tuple-element.127), kind=kOutput, calls=%fused_computation.60.clone.1 | convolution fusion | flops 1245711360 | bytes 19866624 | tf_op jit(solution)/shard_map/while/body/eval_jaxpr/sub | solution.py:93
  378.5 6.7 %fusion.83 = bf16[2,1024,2,96]{1,3,2,0:T(8,128)(2,1)S(1)} fusion(bf16[2,1024,2,96]{1,3,2,0:T(8,128)(2,1)S(1)} %copy-done.9, s32[]{:T(128)} %get-tuple-element.115, bf16[2,1024,3072]{1,2,0:T(8,128)(2,1)} %get-tuple-element.106, bf16[2,3072,96]{1,2,0:T(8,128)(2,1)S(1)} %get-tuple-element.124, f32[1024,2]{0,1:T(2,128)S(1)} %bitcast.127), kind=kOutput, calls=%fused_computation.13.clone.1 | convolution fusion | flops 1208156160 | bytes 13968384 | tf_op jit(solution)/shard_map/while/body/eval_jaxpr/gqk,kd->qgd/dot_general | solution.py:95
  385.2 0.0 copy-start.10
  385.2 0.9 copy-done.10
  386.1 0.0 all-gather.8.cloned.1.call-update
  386.1 0.3 convert_element_type.62
  386.4 0.8 copy.41
  387.2 48.5 %all-to-all-start.3 = ((bf16[4,256,192]{1,2,0:T(8,128)(2,1)}), bf16[4,256,192]{1,2,0:T(8,128)(2,1)S(1)}, u32[]{:S(2)}, u32[]{:S(2)}) async-start(bf16[4,256,192]{1,2,0:T(8,128)(2,1)} %copy.41), calls=%async_computation.3 | async-start | bytes 786432 | tf_op jit(solution)/shard_map/all_to_all | solution.py:64
  435.7 0.8 copy.48
  436.5 7.3 %all-to-all-done.3 = bf16[4,256,192]{1,2,0:T(8,128)(2,1)S(1)} async-done(((bf16[4,256,192]{1,2,0:T(8,128)(2,1)}), bf16[4,256,192]{1,2,0:T(8,128)(2,1)S(1)}, u32[]{:S(2)}, u32[]{:S(2)}) %all-to-all-start.3) | async-done | bytes 393248 | tf_op jit(solution)/shard_map/all_to_all | solution.py:64
  443.8 4.3 all-to-all-start.4
  448.1 18.9 %all-gather.8.cloned.1.call-done = bf16[1024,1536]{0,1:T(8,128)(2,1)} async-done(((bf16[1024,384]{0,1:T(8,128)(2,1)}), bf16[1024,1536]{0,1:T(8,128)(2,1)}) %all-gather.8.cloned.1.call-update) | async-done | bytes 3145744 | tf_op jit(solution)/shard_map/all_gather | solution.py:109
  467.0 4.9 convolution_convert_fusion
  471.9 0.0 all-to-all-done.4
  471.9 3.7 all-to-all-start.2
  475.7 0.9 copy.43
  476.6 0.9 copy.44
  477.5 10.5 %all-to-all-done.2 = bf16[4,256,384]{2,1,0:T(8,128)(2,1)S(1)} async-done(((bf16[4,256,384]{2,1,0:T(8,128)(2,1)}), bf16[4,256,384]{2,1,0:T(8,128)(2,1)S(1)}, u32[]{:S(2)}, u32[]{:S(2)}) %all-to-all-start.2) | async-done | bytes 786464 | tf_op jit(solution)/shard_map/all_to_all | solution.py:113
  488.0 0.6 copy.40
  488.6 1.2 broadcast_in_dim.58
  (30 shorter events, 0.1 us)
Async XLA Ops:
  7.2 4.6 copy-start.11
  7.2 4.6 copy-start.13
  7.2 4.6 copy-start.14
  7.2 4.6 copy-start.12
  7.2 5.4 %copy-start.7 = (bf16[1,512,768]{2,1,0:T(8,128)(2,1)S(1)}, bf16[1,512,768]{2,1,0:T(8,128)(2,1)}, u32[]{:S(2)}) copy-start(bf16[1,512,768]{2,1,0:T(8,128)(2,1)} %param.13) | copy-start | bytes 2359300
  7.2 53.3 %all-gather.4.cloned.1.call-start = ((), (), s32[]{:S(2)}) async-start(), calls=%async_computation.5 | async-start | bytes 3932160 | tf_op jit(solution)/shard_map/all_gather | solution.py:50
  8.0 13.1 %copy-start.8 = (bf16[1,512,768]{2,1,0:T(8,128)(2,1)S(1)}, bf16[1,512,768]{2,1,0:T(8,128)(2,1)}, u32[]{:S(2)}) copy-start(bf16[1,512,768]{2,1,0:T(8,128)(2,1)} %param.14) | copy-start | bytes 2359300
  11.8 307.8 %all-gather.6.cloned.1.call-start = ((), (), s32[]{:S(2)}) async-start(), calls=%async_computation.6 | async-start | bytes 3594240 | tf_op jit(solution)/shard_map/all_gather | solution.py:52
  13.8 19.0 %all-to-all-start.1 = ((bf16[512,4,192]{0,2,1:T(8,128)(2,1)}), bf16[512,4,192]{0,2,1:T(8,128)(2,1)S(1)}, u32[]{:S(2)}, u32[]{:S(2)}) async-start(bf16[512,4,192]{0,2,1:T(8,128)(2,1)} %bitcast.16), calls=%async_computation.1 | async-start | bytes 1572864 | tf_op jit(solution)/shard_map/all_to_all | solution.py:66
  32.8 25.6 %all-to-all-start = ((bf16[512,4,192]{0,2,1:T(8,128)(2,1)}), bf16[512,4,192]{0,2,1:T(8,128)(2,1)S(1)}, u32[]{:S(2)}, u32[]{:S(2)}) async-start(bf16[512,4,192]{0,2,1:T(8,128)(2,1)} %bitcast.9), calls=%async_computation | async-start | bytes 1572864 | tf_op jit(solution)/shard_map/all_to_all | solution.py:67
  38.0 429.0 %all-gather.8.cloned.1.call-start = ((), (), s32[]{:S(2)}) async-start(), calls=%async_computation.7 | async-start | bytes 3932160 | tf_op jit(solution)/shard_map/all_gather | solution.py:109
  60.5 262.3 %copy-start.3 = (f32[1024,48]{0,1:T(8,128)S(1)}, f32[1024,48]{0,1:T(8,128)}, u32[]{:S(2)}) copy-start(f32[1024,48]{0,1:T(8,128)} %get-tuple-element.63) | copy-start | bytes 589828
  60.5 262.3 %copy-start.4 = (f32[1024,48]{0,1:T(8,128)S(1)}, f32[1024,48]{0,1:T(8,128)}, u32[]{:S(2)}) copy-start(f32[1024,48]{0,1:T(8,128)} %get-tuple-element.64) | copy-start | bytes 589828
  60.5 262.5 %copy-start = (bf16[1024,1536]{1,0:T(8,128)(2,1)S(1)}, bf16[1024,1536]{1,0:T(8,128)(2,1)}, u32[]{:S(2)}) copy-start(bf16[1024,1536]{1,0:T(8,128)(2,1)} %all-gather.4.cloned.1.call-done) | copy-start | bytes 9437188
  325.7 1.1 copy-start.1
  327.9 3.6 copy-start.2
  331.5 0.8 copy-start.5
  332.3 19.3 %copy-start.9 = (bf16[2,1024,2,96]{1,3,2,0:T(8,128)(2,1)S(1)}, bf16[2,1024,2,96]{1,3,2,0:T(8,128)(2,1)}, u32[]{:S(2)}) copy-start(bf16[2,1024,2,96]{1,3,2,0:T(8,128)(2,1)} %get-tuple-element.116) | copy-start | bytes 2359300 | tf_op jit(solution)/shard_map/while
  358.3 0.9 copy-start.10
  359.2 19.3 %copy-start.9 = (bf16[2,1024,2,96]{1,3,2,0:T(8,128)(2,1)S(1)}, bf16[2,1024,2,96]{1,3,2,0:T(8,128)(2,1)}, u32[]{:S(2)}) copy-start(bf16[2,1024,2,96]{1,3,2,0:T(8,128)(2,1)} %get-tuple-element.116) | copy-start | bytes 2359300 | tf_op jit(solution)/shard_map/while
  385.2 0.9 copy-start.10
  386.1 49.6 %copy-start.6 = (bf16[1024,192]{0,1:T(8,128)(2,1)S(1)}, bf16[1024,192]{0,1:T(8,128)(2,1)}, u32[]{:S(2)}) copy-start(bf16[1024,192]{0,1:T(8,128)(2,1)} %copy-done.5) | copy-start | bytes 1179652
  387.2 56.6 %all-to-all-start.3 = ((bf16[4,256,192]{1,2,0:T(8,128)(2,1)}), bf16[4,256,192]{1,2,0:T(8,128)(2,1)S(1)}, u32[]{:S(2)}, u32[]{:S(2)}) async-start(bf16[4,256,192]{1,2,0:T(8,128)(2,1)} %copy.41), calls=%async_computation.3 | async-start | bytes 786432 | tf_op jit(solution)/shard_map/all_to_all | solution.py:64
  443.8 28.2 %all-to-all-start.4 = ((bf16[4,256,192]{1,2,0:T(8,128)(2,1)}), bf16[4,256,192]{1,2,0:T(8,128)(2,1)S(1)}, u32[]{:S(2)}, u32[]{:S(2)}) async-start(bf16[4,256,192]{1,2,0:T(8,128)(2,1)} %bitcast.97), calls=%async_computation.4 | async-start | bytes 786432 | tf_op jit(solution)/shard_map/all_to_all | solution.py:65
  471.9 16.0 %all-to-all-start.2 = ((bf16[4,256,384]{2,1,0:T(8,128)(2,1)}), bf16[4,256,384]{2,1,0:T(8,128)(2,1)S(1)}, u32[]{:S(2)}, u32[]{:S(2)}) async-start(bf16[4,256,384]{2,1,0:T(8,128)(2,1)} %bitcast.25), calls=%async_computation.2 | async-start | bytes 1572864 | tf_op jit(solution)/shard_map/all_to_all | solution.py:113
Sparse Core Ops, SparseCore 0:
  11.9 47.5 all-gather.3
  61.2 258.2 all-gather.5
  386.2 80.7 all-gather.7
where the time goes:
time: 497 us; the launch traced here: 496 us
  waiting for transfers between devices  319 us (64%)
  starting transfers between devices  68.6 us (14%)
  matrix products  65.6 us (13%)
  local copies, waits for them, and re-layouts  16 us (3%)
  between operations  14.6 us (3%)
  other arithmetic  12.3 us (2%)
    all_gather x1, waiting for transfers between devices, body(): cols = lax.all_gather(pieces, 'req', axis=0, tiled=True)  259 us
    all_to_all x1, starting transfers between devices, body(): lax.all_to_all(keys_new, 'kv', split_axis=0, concat_axis=1, tiled=True)  48.5 us
    sub x2, matrix products, attend(): weights = jnp.where(visible[None], jnp.exp(score - peak[..., None]), 0.0)  38.6 us
    all_gather x1, waiting for transfers between devices, body(): context_all = lax.all_gather(context, 'kv', axis=1, tiled=True)  18.9 us
    all_to_all x1, waiting for transfers between devices, body(): lax.all_to_all(value_cache[0], 'kv', split_axis=1, concat_axis=0, tiled=T...  14.8 us
    dot_general x2, matrix products, attend(): jnp.einsum('gqk,kd->qgd', weights.astype(jnp.bfloat16), value_block, pref...  13.4 us
    all_to_all x1, waiting for transfers between devices, body(): lax.all_to_all(attended_cols, 'kv', split_axis=0, concat_axis=1, tiled=True)  10.5 us
  transfers between devices with their start and end apart: 8, of which 6 were waited for; matrix products, arithmetic and copies ran while one was open for 4% of the time, Pallas kernels for 0%

commit v1 on v0

--- a/solution.py
+++ b/solution.py
@@ -49,7 +49,9 @@
     normed = rms_norm(hidden[0].astype(jnp.float32), norm_gain)
     normed_all = lax.all_gather(normed, "kv", axis=0, tiled=True)
     pieces = jnp.concatenate([w_query, w_key, w_value, w_out], axis=1)
-    cols = lax.all_gather(pieces, "req", axis=0, tiled=True)
+    cols = jnp.concatenate(
+        lax.all_to_all(jnp.stack([pieces] * lax.axis_size("req")), "req", 0, 0), axis=0
+    )
     wq = cols[:, :q_cols]
     wk = cols[:, q_cols : q_cols + k_cols]
     wv = cols[:, q_cols + k_cols : q_cols + k_cols + v_cols]

time: 497 us -> 273 us (0.55)
  waiting for transfers between devices: 319 us -> 112 us
  starting transfers between devices: 68.6 us -> 39.1 us
  local copies, waits for them, and re-layouts: 16 us -> 27.7 us
    all_gather x1 -> x0, waiting for transfers between devices: 259 us -> none  [body(): cols = lax.all_gather(pieces, 'req', axis=0, tiled=True)]
    all_to_all x1, starting transfers between devices: 48.5 us -> 7.84 us  [body(): lax.all_to_all(keys_new, 'kv', split_axis=0, concat_axis=1, tiled=True)]
    all_gather x1, waiting for transfers between devices: 0.01 us -> 33.5 us  [body(): normed_all = lax.all_gather(normed, 'kv', axis=0, tiled=True)]
    all_to_all x0 -> x1, waiting for transfers between devices: none -> 26.2 us  [body(): lax.all_to_all(jnp.stack([pieces] * lax.axis_size('req')), 'req', 0, 0)]
    all_to_all x0 -> x1, starting transfers between devices: none -> 11.2 us  [body(): lax.all_to_all(jnp.stack([pieces] * lax.axis_size('req')), 'req', 0, 0)]
    all_gather x1, waiting for transfers between devices: 18.9 us -> 9.6 us  [body(): context_all = lax.all_gather(context, 'kv', axis=1, tiled=True)]
  transfers between devices with their start and end apart: 8 -> 8, of which waited for: 6 -> 7; matrix products, arithmetic and copies ran while one was open for 4% -> 13% of each run, Pallas kernels for 0% -> 0%
where the time goes in v1:
time: 273 us; the launch traced here: 271 us
  waiting for transfers between devices  112 us (41%)
  matrix products  64.5 us (24%)
  starting transfers between devices  39.1 us (14%)
  local copies, waits for them, and re-layouts  27.7 us (10%)
  between operations  14.9 us (5%)
  other arithmetic  12.6 us (5%)
    sub x2, matrix products, attend(): weights = jnp.where(visible[None], jnp.exp(score - peak[..., None]), 0.0)  38.5 us
    all_gather x1, waiting for transfers between devices, body(): normed_all = lax.all_gather(normed, 'kv', axis=0, tiled=True)  33.5 us
    all_to_all x1, waiting for transfers between devices, body(): lax.all_to_all(jnp.stack([pieces] * lax.axis_size('req')), 'req', 0, 0)  26.2 us
    dot_general x2, matrix products, attend(): jnp.einsum('gqk,kd->qgd', weights.astype(jnp.bfloat16), value_block, pref...  15.3 us
    all_to_all x1, waiting for transfers between devices, body(): lax.all_to_all(value_cache[0], 'kv', split_axis=1, concat_axis=0, tiled=T...  12.2 us
    all_to_all x1, starting transfers between devices, body(): lax.all_to_all(jnp.stack([pieces] * lax.axis_size('req')), 'req', 0, 0)  11.2 us
    all_to_all x1, waiting for transfers between devices, body(): lax.all_to_all(key_cache[0], 'kv', split_axis=1, concat_axis=0, tiled=True)  11.1 us
    all_to_all x1, waiting for transfers between devices, body(): lax.all_to_all(keys_new, 'kv', split_axis=0, concat_axis=1, tiled=True)  10.8 us
  transfers between devices with their start and end apart: 8, of which 7 were waited for; matrix products, arithmetic and copies ran while one was open for 13% of the time, Pallas kernels for 0%

profile of v1, /device:TPU:1, one launch (start us, length us, event | category | flops | bytes accessed | tf_op | source)
XLA Modules:
  0.0 270.8 jit_solution(11472854711332432233)
XLA Ops:
  7.2 0.0 copy-start.10
  7.2 0.0 copy-start.11
  7.2 0.0 copy-start.13
  7.2 0.0 copy-start.14
  7.2 0.0 copy-start.12
  7.2 2.4 copy.38
  9.6 6.7 %all-to-all-start.2 = ((bf16[512,4,192]{0,2,1:T(8,128)(2,1)}), bf16[512,4,192]{0,2,1:T(8,128)(2,1)S(1)}, u32[]{:S(2)}, u32[]{:S(2)}) async-start(bf16[512,4,192]{0,2,1:T(8,128)(2,1)} %bitcast.17), calls=%async_computation.2 | async-start | bytes 1572864 | tf_op jit(solution)/shard_map/all_to_all | solution.py:68
  16.3 0.0 copy-done.10
  16.3 1.2 copy.36
  17.5 11.1 %all-to-all-done.2 = bf16[512,4,192]{0,2,1:T(8,128)(2,1)S(1)} async-done(((bf16[512,4,192]{0,2,1:T(8,128)(2,1)}), bf16[512,4,192]{0,2,1:T(8,128)(2,1)S(1)}, u32[]{:S(2)}, u32[]{:S(2)}) %all-to-all-start.2) | async-done | bytes 786464 | tf_op jit(solution)/shard_map/all_to_all | solution.py:68
  28.6 4.3 %all-to-all-start = ((bf16[512,4,192]{0,2,1:T(8,128)(2,1)}), bf16[512,4,192]{0,2,1:T(8,128)(2,1)S(1)}, u32[]{:S(2)}, u32[]{:S(2)}) async-start(bf16[512,4,192]{0,2,1:T(8,128)(2,1)} %bitcast.9), calls=%async_computation | async-start | bytes 1572864 | tf_op jit(solution)/shard_map/all_to_all | solution.py:69
  32.9 0.0 copy-done.12
  32.9 0.1 concatenate.28
  33.0 12.2 %all-to-all-done = bf16[512,4,192]{0,2,1:T(8,128)(2,1)S(1)} async-done(((bf16[512,4,192]{0,2,1:T(8,128)(2,1)}), bf16[512,4,192]{0,2,1:T(8,128)(2,1)S(1)}, u32[]{:S(2)}, u32[]{:S(2)}) %all-to-all-start) | async-done | bytes 786464 | tf_op jit(solution)/shard_map/all_to_all | solution.py:69
  45.2 2.0 stack.2
  47.2 0.0 copy-done.4
  47.2 11.2 %all-to-all-start.1 = ((bf16[64,24,1152]{2,1,0:T(8,128)(2,1)}), bf16[64,24,1152]{2,1,0:T(8,128)(2,1)S(1)}, u32[]{:S(2)}, u32[]{:S(2)}) async-start(bf16[64,24,1152]{2,1,0:T(8,128)(2,1)} %stack.2), calls=%async_computation.1 | async-start | bytes 7077888 | tf_op jit(solution)/shard_map/all_to_all | solution.py:53
  58.4 0.0 all-gather.3.cloned.1.call-start
  58.5 1.4 fusion.49
  59.9 2.3 fusion.51
  62.1 0.0 all-gather.3.cloned.1.call-update
  62.1 0.2 all-gather.5.cloned.1.call-start
  63.1 0.3 iota_compare_fusion
  63.4 1.5 multiply_cosine_fusion
  64.9 3.5 %pad_add_fusion = pred[1024,3072]{0,1:T(8,128)(4,1)} fusion(pred[1024,1024]{0,1:T(8,128)(4,1)S(1)} %iota_compare_fusion, pred[3072]{0:T(1024)(128)(4,1)S(1)} %pad.6.clone), kind=kLoop, calls=%fused_computation.30 | loop fusion | flops 3145728 | bytes 4197376 | tf_op jit(solution)/shard_map/concatenate | solution.py:76
  68.5 1.6 copy.39
  70.0 2.8 %concatenate.32 = bf16[2048,2,96]{0,2,1:T(8,128)(2,1)} reshape(bf16[4,512,192]{1,0,2:T(4,128)(2,1)} %copy.39) | data formatting | bytes 1572864 | tf_op jit(solution)/shard_map/concatenate | solution.py:71
  72.8 2.8 %copy.37 = bf16[4,512,192]{1,0,2:T(4,128)(2,1)} copy(bf16[4,512,192]{1,2,0:T(8,128)(2,1)} %bitcast.123) | data formatting | bytes 1572864 | tf_op jit(solution)/shard_map/all_to_all | solution.py:69
  75.6 2.9 %concatenate.27 = bf16[2048,2,96]{0,2,1:T(8,128)(2,1)} reshape(bf16[4,512,192]{1,0,2:T(4,128)(2,1)} %copy.37) | data formatting | bytes 1572864 | tf_op jit(solution)/shard_map/concatenate | solution.py:72
  78.4 33.5 %all-gather.3.cloned.1.call-done = bf16[1024,1536]{1,0:T(8,128)(2,1)} async-done(((bf16[256,1536]{1,0:T(8,128)(2,1)}), bf16[1024,1536]{1,0:T(8,128)(2,1)}) %all-gather.3.cloned.1.call-update) | async-done | bytes 3145744 | tf_op jit(solution)/shard_map/all_gather | solution.py:50
  112.0 26.2 %all-to-all-done.1 = bf16[64,24,1152]{2,1,0:T(8,128)(2,1)S(1)} async-done(((bf16[64,24,1152]{2,1,0:T(8,128)(2,1)}), bf16[64,24,1152]{2,1,0:T(8,128)(2,1)S(1)}, u32[]{:S(2)}, u32[]{:S(2)}) %all-to-all-start.1) | async-done | bytes 3538976 | tf_op jit(solution)/shard_map/all_to_all | solution.py:53
  138.2 3.2 %fusion.55 = f32[1024,192]{0,1:T(8,128)S(1)} fusion(bf16[1024,1536]{1,0:T(8,128)(2,1)} %all-gather.3.cloned.1.call-done, bf16[1536,1152]{1,0:T(8,128)(2,1)S(1)} %bitcast.117), kind=kOutput, calls=%fused_computation.44 | convolution fusion | flops 603979776 | bytes 4718592 | tf_op jit(solution)/shard_map/dot_general | solution.py:61
  141.5 0.1 multiply_subtract_fusion
  141.6 1.5 fusion.53
  143.1 0.0 copy-start.6
  143.1 0.3 subtract_convert_fusion
  143.4 0.0 copy-start
  143.4 0.7 copy-done
  144.2 0.1 copy-done.6
  144.2 1.1 maximum_bitcast_fusion.1
  145.3 0.9 pad_maximum_fusion
  146.3 1.4 convolution_convert_fusion.1
  147.7 1.2 maximum_bitcast_fusion
  148.9 53.8 %while.10 = (s32[]{:T(128)}, bf16[2,1024,2,96]{1,3,2,0:T(8,128)(2,1)}, bf16[2,3072,96]{1,2,0:T(8,128)(2,1)}, pred[1024,3072]{0,1:T(8,128)(4,1)}, bf16[2,3072,96]...) while((s32[]{:T(128)}, bf16[2,1024,2,96]{1,3,2,0:T(8,128)(2,1)}, ...), condition=%wide.region_4.5_spmd, body=%wide.region_1.4_spmd.sunk | while | flops 2453867520 | bytes 33835084 | solution.py:105
  148.9 19.2 %fusion.82 = (f32[2,1024]{1,0:T(2,128)S(1)}, bf16[2,1024,3072]{1,2,0:T(8,128)(2,1)}) fusion(pred[1024,3072]{0,1:T(8,128)(4,1)} %get-tuple-element.125, bf16[2,3072,96]{1,2,0:T(8,128)(2,1)} %get-tuple-element.126, s32[]{:T(128)} %get-tuple-element.115, bf16[2,1024,2,96]{1,3,2,0:T(8,128)(2,1)} %get-tuple-element.127), kind=kOutput, calls=%fused_computation.60.clone.1 | convolution fusion | flops 1245711360 | bytes 19866624 | tf_op jit(solution)/shard_map/while/body/eval_jaxpr/sub | solution.py:95
  168.1 7.6 %fusion.83 = bf16[2,1024,2,96]{1,3,2,0:T(8,128)(2,1)} fusion(bf16[2,1024,2,96]{1,3,2,0:T(8,128)(2,1)} %get-tuple-element.116, s32[]{:T(128)} %get-tuple-element.115, bf16[2,1024,3072]{1,2,0:T(8,128)(2,1)} %get-tuple-element.106, bf16[2,3072,96]{1,2,0:T(8,128)(2,1)} %get-tuple-element.124, f32[1024,2]{0,1:T(2,128)S(1)} %bitcast.132), kind=kOutput, calls=%fused_computation.13.clone.1 | convolution fusion | flops 1208156160 | bytes 13968384 | tf_op jit(solution)/shard_map/while/body/eval_jaxpr/gqk,kd->qgd/dot_general | solution.py:97
  175.7 19.3 %fusion.82 = (f32[2,1024]{1,0:T(2,128)S(1)}, bf16[2,1024,3072]{1,2,0:T(8,128)(2,1)}) fusion(pred[1024,3072]{0,1:T(8,128)(4,1)} %get-tuple-element.125, bf16[2,3072,96]{1,2,0:T(8,128)(2,1)} %get-tuple-element.126, s32[]{:T(128)} %get-tuple-element.115, bf16[2,1024,2,96]{1,3,2,0:T(8,128)(2,1)} %get-tuple-element.127), kind=kOutput, calls=%fused_computation.60.clone.1 | convolution fusion | flops 1245711360 | bytes 19866624 | tf_op jit(solution)/shard_map/while/body/eval_jaxpr/sub | solution.py:95
  195.0 7.6 %fusion.83 = bf16[2,1024,2,96]{1,3,2,0:T(8,128)(2,1)} fusion(bf16[2,1024,2,96]{1,3,2,0:T(8,128)(2,1)} %get-tuple-element.116, s32[]{:T(128)} %get-tuple-element.115, bf16[2,1024,3072]{1,2,0:T(8,128)(2,1)} %get-tuple-element.106, bf16[2,3072,96]{1,2,0:T(8,128)(2,1)} %get-tuple-element.124, f32[1024,2]{0,1:T(2,128)S(1)} %bitcast.132), kind=kOutput, calls=%fused_computation.13.clone.1 | convolution fusion | flops 1208156160 | bytes 13968384 | tf_op jit(solution)/shard_map/while/body/eval_jaxpr/gqk,kd->qgd/dot_general | solution.py:97
  202.6 0.0 all-gather.5.cloned.1.call-update
  202.7 2.0 convert_element_type.62
  204.7 1.8 copy.41
  206.5 7.8 %all-to-all-start.4 = ((bf16[4,256,192]{1,2,0:T(8,128)(2,1)}), bf16[4,256,192]{1,2,0:T(8,128)(2,1)}, u32[]{:S(2)}, u32[]{:S(2)}) async-start(bf16[4,256,192]{1,2,0:T(8,128)(2,1)} %copy.41), calls=%async_computation.4 | async-start | bytes 786432 | tf_op jit(solution)/shard_map/all_to_all | solution.py:66
  214.3 1.8 copy.48
  216.1 10.8 %all-to-all-done.4 = bf16[4,256,192]{1,2,0:T(8,128)(2,1)} async-done(((bf16[4,256,192]{1,2,0:T(8,128)(2,1)}), bf16[4,256,192]{1,2,0:T(8,128)(2,1)}, u32[]{:S(2)}, u32[]{:S(2)}) %all-to-all-start.4) | async-done | bytes 393248 | tf_op jit(solution)/shard_map/all_to_all | solution.py:66
  226.9 5.1 %all-to-all-start.5 = ((bf16[4,256,192]{1,2,0:T(8,128)(2,1)}), bf16[4,256,192]{1,2,0:T(8,128)(2,1)}, u32[]{:S(2)}, u32[]{:S(2)}) async-start(bf16[4,256,192]{1,2,0:T(8,128)(2,1)} %bitcast.127), calls=%async_computation.5 | async-start | bytes 786432 | tf_op jit(solution)/shard_map/all_to_all | solution.py:67
  232.0 9.6 %all-gather.5.cloned.1.call-done = bf16[1024,1536]{0,1:T(8,128)(2,1)} async-done(((bf16[1024,384]{0,1:T(8,128)(2,1)}), bf16[1024,1536]{0,1:T(8,128)(2,1)}) %all-gather.5.cloned.1.call-update) | async-done | bytes 3145744 | tf_op jit(solution)/shard_map/all_gather | solution.py:111
  241.6 4.6 %convolution_convert_fusion = bf16[1024,384]{1,0:T(8,128)(2,1)} fusion(bf16[1024,1536]{0,1:T(8,128)(2,1)} %all-gather.5.cloned.1.call-done, bf16[1536,1152]{1,0:T(8,128)(2,1)S(1)} %bitcast.120), kind=kOutput, calls=%fused_computation.37 | convolution fusion | flops 1208352768 | bytes 5111808 | tf_op jit(solution)/shard_map/dot_general | solution.py:112
  246.2 0.0 all-to-all-done.5
  246.2 3.7 %all-to-all-start.3 = ((bf16[4,256,384]{2,1,0:T(8,128)(2,1)}), bf16[4,256,384]{2,1,0:T(8,128)(2,1)S(1)}, u32[]{:S(2)}, u32[]{:S(2)}) async-start(bf16[4,256,384]{2,1,0:T(8,128)(2,1)} %bitcast.131), calls=%async_computation.3 | async-start | bytes 1572864 | tf_op jit(solution)/shard_map/all_to_all | solution.py:115
  249.9 1.9 copy.43
  251.8 1.9 copy.44
  253.7 8.5 %all-to-all-done.3 = bf16[4,256,384]{2,1,0:T(8,128)(2,1)S(1)} async-done(((bf16[4,256,384]{2,1,0:T(8,128)(2,1)}), bf16[4,256,384]{2,1,0:T(8,128)(2,1)S(1)}, u32[]{:S(2)}, u32[]{:S(2)}) %all-to-all-start.3) | async-done | bytes 786464 | tf_op jit(solution)/shard_map/all_to_all | solution.py:115
  262.2 0.6 copy.40
  262.8 1.2 broadcast_in_dim.58
  (28 shorter events, 0.1 us)
Async XLA Ops:
  7.2 9.1 %copy-start.10 = (bf16[1,512,768]{2,1,0:T(8,128)(2,1)S(1)}, bf16[1,512,768]{2,1,0:T(8,128)(2,1)}, u32[]{:S(2)}) copy-start(bf16[1,512,768]{2,1,0:T(8,128)(2,1)} %param.14) | copy-start | bytes 2359300
  7.2 25.8 %copy-start.11 = (bf16[24,384]{1,0:T(8,128)(2,1)S(1)}, bf16[24,384]{1,0:T(8,128)(2,1)}, u32[]{:S(2)}) copy-start(bf16[24,384]{1,0:T(8,128)(2,1)} %param.16) | copy-start | bytes 55300
  7.2 25.7 %copy-start.13 = (bf16[24,192]{1,0:T(8,128)(2,1)S(1)}, bf16[24,192]{1,0:T(8,128)(2,1)}, u32[]{:S(2)}) copy-start(bf16[24,192]{1,0:T(8,128)(2,1)} %param.17) | copy-start | bytes 27652
  7.2 25.7 %copy-start.14 = (bf16[24,192]{1,0:T(8,128)(2,1)S(1)}, bf16[24,192]{1,0:T(8,128)(2,1)}, u32[]{:S(2)}) copy-start(bf16[24,192]{1,0:T(8,128)(2,1)} %param.18) | copy-start | bytes 27652
  7.2 25.7 %copy-start.12 = (bf16[24,384]{1,0:T(8,128)(2,1)S(1)}, bf16[24,384]{1,0:T(8,128)(2,1)}, u32[]{:S(2)}) copy-start(bf16[24,384]{1,0:T(8,128)(2,1)} %param.19) | copy-start | bytes 55300
  9.6 19.0 %all-to-all-start.2 = ((bf16[512,4,192]{0,2,1:T(8,128)(2,1)}), bf16[512,4,192]{0,2,1:T(8,128)(2,1)S(1)}, u32[]{:S(2)}, u32[]{:S(2)}) async-start(bf16[512,4,192]{0,2,1:T(8,128)(2,1)} %bitcast.17), calls=%async_computation.2 | async-start | bytes 1572864 | tf_op jit(solution)/shard_map/all_to_all | solution.py:68
  28.6 18.6 %copy-start.2 = (bf16[512,4,192]{0,2,1:T(8,128)(2,1)}, bf16[512,4,192]{0,2,1:T(8,128)(2,1)S(1)}, u32[]{:S(2)}) copy-start(bf16[512,4,192]{0,2,1:T(8,128)(2,1)S(1)} %all-to-all-done.2) | copy-start | bytes 2359300
  28.6 16.6 %all-to-all-start = ((bf16[512,4,192]{0,2,1:T(8,128)(2,1)}), bf16[512,4,192]{0,2,1:T(8,128)(2,1)S(1)}, u32[]{:S(2)}, u32[]{:S(2)}) async-start(bf16[512,4,192]{0,2,1:T(8,128)(2,1)} %bitcast.9), calls=%async_computation | async-start | bytes 1572864 | tf_op jit(solution)/shard_map/all_to_all | solution.py:69
  45.2 2.0 copy-start.4
  47.2 11.2 %copy-start.15 = (bf16[1536]{0:T(1024)(128)(2,1)S(1)}, bf16[1536]{0:T(1024)(128)(2,1)}, u32[]{:S(2)}) copy-start(bf16[1536]{0:T(1024)(128)(2,1)} %param.15) | copy-start | bytes 9220
  47.2 91.0 %all-to-all-start.1 = ((bf16[64,24,1152]{2,1,0:T(8,128)(2,1)}), bf16[64,24,1152]{2,1,0:T(8,128)(2,1)S(1)}, u32[]{:S(2)}, u32[]{:S(2)}) async-start(bf16[64,24,1152]{2,1,0:T(8,128)(2,1)} %stack.2), calls=%async_computation.1 | async-start | bytes 7077888 | tf_op jit(solution)/shard_map/all_to_all | solution.py:53
  58.4 53.6 %all-gather.3.cloned.1.call-start = ((), (), s32[]{:S(2)}) async-start(), calls=%async_computation.6 | async-start | bytes 3932160 | tf_op jit(solution)/shard_map/all_gather | solution.py:50
  62.1 179.4 %all-gather.5.cloned.1.call-start = ((), (), s32[]{:S(2)}) async-start(), calls=%async_computation.7 | async-start | bytes 3932160 | tf_op jit(solution)/shard_map/all_gather | solution.py:111
  63.0 5.4 %copy-start.3 = (bf16[512,4,192]{0,2,1:T(8,128)(2,1)S(1)}, bf16[512,4,192]{0,2,1:T(8,128)(2,1)}, u32[]{:S(2)}) copy-start(bf16[512,4,192]{0,2,1:T(8,128)(2,1)} %copy-done.2) | copy-start | bytes 2359300
  138.2 3.2 %copy-start.7 = (f32[1024,48]{0,1:T(8,128)S(1)}, f32[1024,48]{0,1:T(8,128)}, u32[]{:S(2)}) copy-start(f32[1024,48]{0,1:T(8,128)} %get-tuple-element.63) | copy-start | bytes 589828
  138.2 3.2 %copy-start.8 = (f32[1024,48]{0,1:T(8,128)S(1)}, f32[1024,48]{0,1:T(8,128)}, u32[]{:S(2)}) copy-start(f32[1024,48]{0,1:T(8,128)} %get-tuple-element.64) | copy-start | bytes 589828
  138.2 3.4 %copy-start.1 = (bf16[1024,1536]{1,0:T(8,128)(2,1)S(1)}, bf16[1024,1536]{1,0:T(8,128)(2,1)}, u32[]{:S(2)}) copy-start(bf16[1024,1536]{1,0:T(8,128)(2,1)} %all-gather.3.cloned.1.call-done) | copy-start | bytes 9437188
  143.1 1.1 copy-start.6
  143.4 0.7 copy-start
  145.3 2.4 copy-start.5
  147.7 1.2 copy-start.9
  206.5 20.4 %all-to-all-start.4 = ((bf16[4,256,192]{1,2,0:T(8,128)(2,1)}), bf16[4,256,192]{1,2,0:T(8,128)(2,1)}, u32[]{:S(2)}, u32[]{:S(2)}) async-start(bf16[4,256,192]{1,2,0:T(8,128)(2,1)} %copy.41), calls=%async_computation.4 | async-start | bytes 786432 | tf_op jit(solution)/shard_map/all_to_all | solution.py:66
  226.9 19.3 %all-to-all-start.5 = ((bf16[4,256,192]{1,2,0:T(8,128)(2,1)}), bf16[4,256,192]{1,2,0:T(8,128)(2,1)}, u32[]{:S(2)}, u32[]{:S(2)}) async-start(bf16[4,256,192]{1,2,0:T(8,128)(2,1)} %bitcast.127), calls=%async_computation.5 | async-start | bytes 786432 | tf_op jit(solution)/shard_map/all_to_all | solution.py:67
  246.2 16.0 %all-to-all-start.3 = ((bf16[4,256,384]{2,1,0:T(8,128)(2,1)}), bf16[4,256,384]{2,1,0:T(8,128)(2,1)S(1)}, u32[]{:S(2)}, u32[]{:S(2)}) async-start(bf16[4,256,384]{2,1,0:T(8,128)(2,1)} %bitcast.131), calls=%async_computation.3 | async-start | bytes 1572864 | tf_op jit(solution)/shard_map/all_to_all | solution.py:115
Sparse Core Ops, SparseCore 0:
  62.3 49.6 all-gather.2
  202.8 38.7 all-gather.4
